TPU v7x, 32 devices: a whole 2x2x4 slice. The times are simulated.
32 devices in a mesh: freq: 2 (over y), space: 16 (over z, x, core).
Axes of the slice: x: 2, y: 2, z: 4, core: 2. Of those that a mesh axis runs over, the one named last changes fastest.
Arguments:
- probes: float32 [2, 32, 128, 128], P(None, 'space'), may hold values from -6 to 6
- background: float32 [2, 2, 32, 128, 128], P('freq', None, 'space'), may hold values from -6 to 6
- medium: float32 [32, 128, 128], P('space'), may hold values from 0.5 to 2
- shifts: float32 [2, 2], P('freq'), may hold values from -1.25 to 1, as said below
- receivers: int32 [32, 128, 128], P('space'), may hold values 0 or 1
Outputs:
- hessian: float32 [2, 32, 128, 128], P(None, 'space', 'freq')
Inputs may be any that keep to these rules, and one draw needn't show every extreme that they name: `shifts`: column 0 lies in [-1.25, -0.5], column 1 in [0.2, 1.0].
All inputs are finite; a program needn't handle non-finite values. No bound on the sum of `receivers` on one device may be relied on, other than what follows from the above.
Results may differ from a plain program's by a relative error of at most 0.00002.
Values sent between devices are 32-bit elements; how exact they have to be, the bound alone decides.
A program may use at most 64 MiB of HBM per device.

v0:
```python
import jax
import jax.numpy as jnp
from jax import lax
from jax.sharding import PartitionSpec as P

STEPS = 4


OMEGA_RELAX = 0.8


def padded(cells, sides, width):
    for axis, dim in sides:
        count = lax.axis_size(axis)
        ends = count - 1
        head = lax.slice_in_dim(cells, 0, width, axis=dim)
        tail = lax.slice_in_dim(cells, cells.shape[dim] - width, cells.shape[dim], axis=dim)
        cells = jnp.concatenate(
            [
                lax.ppermute(tail, axis, [(i, (i + 1) % count) for i in range(ends)]),
                cells,
                lax.ppermute(head, axis, [((i + 1) % count, i) for i in range(ends)]),
            ],
            axis=dim,
        )
    return cells


def neighbours(extended):
    center = extended[:, :, 1:-1]
    beside_all = extended[:, :, 2:] + extended[:, :, :-2]
    pad_y_low = ((0, 0), (0, 0), (0, 0), (0, 1), (0, 0))
    pad_y_high = ((0, 0), (0, 0), (0, 0), (1, 0), (0, 0))
    pad_z_low = ((0, 0), (0, 0), (0, 0), (0, 0), (0, 1))
    pad_z_high = ((0, 0), (0, 0), (0, 0), (0, 0), (1, 0))
    beside_all = (
        beside_all
        + jnp.pad(center[:, :, :, 1:], pad_y_low)
        + jnp.pad(center[:, :, :, :-1], pad_y_high)
    )
    beside_all = (
        beside_all
        + jnp.pad(center[:, :, :, :, 1:], pad_z_low)
        + jnp.pad(center[:, :, :, :, :-1], pad_z_high)
    )
    return (center, beside_all)


def sweep_once(extended, factors, source):
    diag_re, diag_im, inv_re, inv_im = factors
    center, beside_all = neighbours(extended)
    resid_re = source[0] - (diag_re * center[0] - diag_im * center[1]) + beside_all[0]
    resid_im = source[1] - (diag_re * center[1] + diag_im * center[0]) + beside_all[1]
    return center + jnp.stack(
        [inv_re * resid_re - inv_im * resid_im, inv_re * resid_im + inv_im * resid_re]
    )


def coefficients(medium, shift_re, shift_im):
    diag_re = 6.0 + shift_re * medium
    diag_im = shift_im * medium
    denom = diag_re * diag_re + diag_im * diag_im
    return (diag_re, diag_im, OMEGA_RELAX * diag_re / denom, -OMEGA_RELAX * diag_im / denom)


def conjugate(factors):
    return (factors[0], -factors[1], factors[2], -factors[3])


def per_device(probes, background, medium, shifts, receivers):
    shift_re = shifts[0, 0]
    shift_im = shifts[0, 1]
    back_re = background[0, 0]
    back_im = background[0, 1]
    scaled_re = shift_re * back_re - shift_im * back_im
    scaled_im = shift_re * back_im + shift_im * back_re
    source = jnp.stack([scaled_re * probes, scaled_im * probes])
    listen = receivers.astype(jnp.float32)
    factors = coefficients(medium, shift_re, shift_im)

    def relax_all(right_side, local_factors):
        iterate = jnp.zeros(right_side.shape, jnp.float32)
        for repeat in range(STEPS):
            extended = padded(iterate, (("space", 2),), 1)
            iterate = sweep_once(extended, local_factors, right_side)
        return iterate

    forward = relax_all(source, factors)
    adjoint_field = relax_all(listen * forward, conjugate(factors))
    terms = scaled_re * adjoint_field[0] + scaled_im * adjoint_field[1]
    return lax.psum_scatter(terms, "freq", scatter_dimension=2, tiled=True)


def solution(mesh):
    in_specs = (
        P(None, "space", None, None),
        P("freq", None, "space", None, None),
        P("space", None, None),
        P("freq", None),
        P("space", None, None),
    )
    out_specs = P(None, "space", "freq", None)
    return jax.shard_map(
        per_device, mesh=mesh, in_specs=in_specs, out_specs=out_specs, check_vma=False
    )
```

profile of v0, /device:TPU:0, one launch (start us, length us, event | category | flops | bytes accessed | tf_op | source)
XLA Modules:
  0.0 110.0 jit_solution(2809796383445488148)
XLA Ops:
  6.6 1.4 %collective-permute-start = (f32[2,2,1,128,128]{4,3,2,1,0:T(8,128)S(1)}, f32[2,2,1,128,128]{4,3,2,1,0:T(8,128)S(1)}, u32[]{:S(2)}, u32[]{:S(2)}) collective-permute-start(f32[2,2,1,128,128]{4,3,2,1,0:T(8,128)S(1)} %broadcast.166), channel_id=1, source_target_pairs={{1,0},{2,1},{3,2},{4,3},{5,4},{6,5},{7,6},{8,7},{9,8},{10,9},{11,1... | collective-permute-start | bytes 786440 | tf_op jit(solution)/shard_map/ppermute | solution.py:22
  8.0 3.0 %collective-permute-start.1 = (f32[2,2,1,128,128]{4,3,2,1,0:T(8,128)S(1)}, f32[2,2,1,128,128]{4,3,2,1,0:T(8,128)S(1)}, u32[]{:S(2)}, u32[]{:S(2)}) collective-permute-start(f32[2,2,1,128,128]{4,3,2,1,0:T(8,128)S(1)} %broadcast.166), channel_id=1, source_target_pairs={{0,1},{1,2},{2,3},{3,4},{4,5},{5,6},{6,7},{7,8},{8,9},{9,10},{10,1... | collective-permute-start | bytes 786440 | tf_op jit(solution)/shard_map/ppermute | solution.py:20
  12.4 0.7 multiply_add_fusion.7
  13.3 1.3 %add_bitcast_fusion.3 = (f32[2,128,128]{2,1,0:T(8,128)S(1)}, f32[2,128,128]{2,1,0:T(8,128)S(1)}) fusion(f32[1,2,2,128,128]{4,3,2,1,0:T(8,128)S(1)} %copy-done.2, f32[]{:T(128)} %bitcast.1, f32[]{:T(128)} %bitcast), kind=kLoop, calls=%fused_computation.145 | loop fusion | flops 196608 | bytes 524296 | tf_op jit(solution)/shard_map/add | solution.py:76
  16.0 5.8 %collective-permute-start.3 = (f32[2,2,1,128,128]{4,3,2,1,0:T(8,128)S(1)}, f32[2,2,1,128,128]{4,3,2,1,0:T(8,128)S(1)}, u32[]{:S(2)}, u32[]{:S(2)}) collective-permute-start(f32[2,2,1,128,128]{4,3,2,1,0:T(8,128)S(1)} %get-tuple-element.68), channel_id=1, source_target_pairs={{0,1},{1,2},{2,3},{3,4},{4,5},{5,6},{6,7},{7,8},{8,9},{9,10},{10,1... | collective-permute-start | bytes 786440 | tf_op jit(solution)/shard_map/ppermute | solution.py:20
  21.8 1.3 %collective-permute-start.2 = (f32[2,2,1,128,128]{4,3,2,1,0:T(8,128)S(1)}, f32[2,2,1,128,128]{4,3,2,1,0:T(8,128)S(1)}, u32[]{:S(2)}, u32[]{:S(2)}) collective-permute-start(f32[2,2,1,128,128]{4,3,2,1,0:T(8,128)S(1)} %get-tuple-element.67), channel_id=1, source_target_pairs={{1,0},{2,1},{3,2},{4,3},{5,4},{6,5},{7,6},{8,7},{9,8},{10,9},{11,1... | collective-permute-start | bytes 786440 | tf_op jit(solution)/shard_map/ppermute | solution.py:22
  23.4 3.8 %collective-permute-done.2 = f32[2,2,1,128,128]{4,3,2,1,0:T(8,128)S(1)} collective-permute-done((f32[2,2,1,128,128]{4,3,2,1,0:T(8,128)S(1)}, f32[2,2,1,128,128]{4,3,2,1,0:T(8,128)S(1)}, u32[]{:S(2)}, u32[]{:S(2)}) %collective-permute-start.2) | collective-permute-done | bytes 262176 | tf_op jit(solution)/shard_map/ppermute | solution.py:22
  28.1 6.7 %collective-permute-start.5 = (f32[2,2,1,128,128]{4,3,2,1,0:T(8,128)S(1)}, f32[2,2,1,128,128]{4,3,2,1,0:T(8,128)S(1)}, u32[]{:S(2)}, u32[]{:S(2)}) collective-permute-start(f32[2,2,1,128,128]{4,3,2,1,0:T(8,128)S(1)} %get-tuple-element.62), channel_id=1, source_target_pairs={{0,1},{1,2},{2,3},{3,4},{4,5},{5,6},{6,7},{7,8},{8,9},{9,10},{10,1... | collective-permute-start | bytes 786440 | tf_op jit(solution)/shard_map/ppermute | solution.py:20
  34.8 1.3 %collective-permute-start.4 = (f32[2,2,1,128,128]{4,3,2,1,0:T(8,128)S(1)}, f32[2,2,1,128,128]{4,3,2,1,0:T(8,128)S(1)}, u32[]{:S(2)}, u32[]{:S(2)}) collective-permute-start(f32[2,2,1,128,128]{4,3,2,1,0:T(8,128)S(1)} %get-tuple-element.61), channel_id=1, source_target_pairs={{1,0},{2,1},{3,2},{4,3},{5,4},{6,5},{7,6},{8,7},{9,8},{10,9},{11,1... | collective-permute-start | bytes 786440 | tf_op jit(solution)/shard_map/ppermute | solution.py:22
  36.2 2.0 %collective-permute-done.4 = f32[2,2,1,128,128]{4,3,2,1,0:T(8,128)S(1)} collective-permute-done((f32[2,2,1,128,128]{4,3,2,1,0:T(8,128)S(1)}, f32[2,2,1,128,128]{4,3,2,1,0:T(8,128)S(1)}, u32[]{:S(2)}, u32[]{:S(2)}) %collective-permute-start.4) | collective-permute-done | bytes 262176 | tf_op jit(solution)/shard_map/ppermute | solution.py:22
  39.1 6.9 %collective-permute-start.7 = (f32[2,2,1,128,128]{4,3,2,1,0:T(8,128)S(1)}, f32[2,2,1,128,128]{4,3,2,1,0:T(8,128)S(1)}, u32[]{:S(2)}, u32[]{:S(2)}) collective-permute-start(f32[2,2,1,128,128]{4,3,2,1,0:T(8,128)S(1)} %get-tuple-element.56), channel_id=1, source_target_pairs={{0,1},{1,2},{2,3},{3,4},{4,5},{5,6},{6,7},{7,8},{8,9},{9,10},{10,1... | collective-permute-start | bytes 786440 | tf_op jit(solution)/shard_map/ppermute | solution.py:20
  46.1 1.3 %collective-permute-start.6 = (f32[2,2,1,128,128]{4,3,2,1,0:T(8,128)S(1)}, f32[2,2,1,128,128]{4,3,2,1,0:T(8,128)S(1)}, u32[]{:S(2)}, u32[]{:S(2)}) collective-permute-start(f32[2,2,1,128,128]{4,3,2,1,0:T(8,128)S(1)} %get-tuple-element.55), channel_id=1, source_target_pairs={{1,0},{2,1},{3,2},{4,3},{5,4},{6,5},{7,6},{8,7},{9,8},{10,9},{11,1... | collective-permute-start | bytes 786440 | tf_op jit(solution)/shard_map/ppermute | solution.py:22
  47.5 2.0 %collective-permute-done.6 = f32[2,2,1,128,128]{4,3,2,1,0:T(8,128)S(1)} collective-permute-done((f32[2,2,1,128,128]{4,3,2,1,0:T(8,128)S(1)}, f32[2,2,1,128,128]{4,3,2,1,0:T(8,128)S(1)}, u32[]{:S(2)}, u32[]{:S(2)}) %collective-permute-start.6) | collective-permute-done | bytes 262176 | tf_op jit(solution)/shard_map/ppermute | solution.py:22
  50.3 7.1 %collective-permute-start.9 = (f32[2,2,1,128,128]{4,3,2,1,0:T(8,128)S(1)}, f32[2,2,1,128,128]{4,3,2,1,0:T(8,128)S(1)}, u32[]{:S(2)}, u32[]{:S(2)}) collective-permute-start(f32[2,2,1,128,128]{4,3,2,1,0:T(8,128)S(1)} %get-tuple-element.50), channel_id=1, source_target_pairs={{0,1},{1,2},{2,3},{3,4},{4,5},{5,6},{6,7},{7,8},{8,9},{9,10},{10,1... | collective-permute-start | bytes 786440 | tf_op jit(solution)/shard_map/ppermute | solution.py:20
  57.4 1.3 %collective-permute-start.8 = (f32[2,2,1,128,128]{4,3,2,1,0:T(8,128)S(1)}, f32[2,2,1,128,128]{4,3,2,1,0:T(8,128)S(1)}, u32[]{:S(2)}, u32[]{:S(2)}) collective-permute-start(f32[2,2,1,128,128]{4,3,2,1,0:T(8,128)S(1)} %get-tuple-element.49), channel_id=1, source_target_pairs={{1,0},{2,1},{3,2},{4,3},{5,4},{6,5},{7,6},{8,7},{9,8},{10,9},{11,1... | collective-permute-start | bytes 786440 | tf_op jit(solution)/shard_map/ppermute | solution.py:22
  59.0 1.8 %collective-permute-done.8 = f32[2,2,1,128,128]{4,3,2,1,0:T(8,128)S(1)} collective-permute-done((f32[2,2,1,128,128]{4,3,2,1,0:T(8,128)S(1)}, f32[2,2,1,128,128]{4,3,2,1,0:T(8,128)S(1)}, u32[]{:S(2)}, u32[]{:S(2)}) %collective-permute-start.8) | collective-permute-done | bytes 262176 | tf_op jit(solution)/shard_map/ppermute | solution.py:22
  61.7 7.1 %collective-permute-start.11 = (f32[2,2,1,128,128]{4,3,2,1,0:T(8,128)S(1)}, f32[2,2,1,128,128]{4,3,2,1,0:T(8,128)S(1)}, u32[]{:S(2)}, u32[]{:S(2)}) collective-permute-start(f32[2,2,1,128,128]{4,3,2,1,0:T(8,128)S(1)} %get-tuple-element.44), channel_id=1, source_target_pairs={{0,1},{1,2},{2,3},{3,4},{4,5},{5,6},{6,7},{7,8},{8,9},{9,10},{10,1... | collective-permute-start | bytes 786440 | tf_op jit(solution)/shard_map/ppermute | solution.py:20
  68.8 1.3 %collective-permute-start.10 = (f32[2,2,1,128,128]{4,3,2,1,0:T(8,128)S(1)}, f32[2,2,1,128,128]{4,3,2,1,0:T(8,128)S(1)}, u32[]{:S(2)}, u32[]{:S(2)}) collective-permute-start(f32[2,2,1,128,128]{4,3,2,1,0:T(8,128)S(1)} %get-tuple-element.43), channel_id=1, source_target_pairs={{1,0},{2,1},{3,2},{4,3},{5,4},{6,5},{7,6},{8,7},{9,8},{10,9},{11,1... | collective-permute-start | bytes 786440 | tf_op jit(solution)/shard_map/ppermute | solution.py:22
  70.2 2.0 %collective-permute-done.10 = f32[2,2,1,128,128]{4,3,2,1,0:T(8,128)S(1)} collective-permute-done((f32[2,2,1,128,128]{4,3,2,1,0:T(8,128)S(1)}, f32[2,2,1,128,128]{4,3,2,1,0:T(8,128)S(1)}, u32[]{:S(2)}, u32[]{:S(2)}) %collective-permute-start.10) | collective-permute-done | bytes 262176 | tf_op jit(solution)/shard_map/ppermute | solution.py:22
  73.2 7.1 %collective-permute-start.13 = (f32[2,2,1,128,128]{4,3,2,1,0:T(8,128)S(1)}, f32[2,2,1,128,128]{4,3,2,1,0:T(8,128)S(1)}, u32[]{:S(2)}, u32[]{:S(2)}) collective-permute-start(f32[2,2,1,128,128]{4,3,2,1,0:T(8,128)S(1)} %get-tuple-element.38), channel_id=1, source_target_pairs={{0,1},{1,2},{2,3},{3,4},{4,5},{5,6},{6,7},{7,8},{8,9},{9,10},{10,1... | collective-permute-start | bytes 786440 | tf_op jit(solution)/shard_map/ppermute | solution.py:20
  80.2 1.3 %collective-permute-start.12 = (f32[2,2,1,128,128]{4,3,2,1,0:T(8,128)S(1)}, f32[2,2,1,128,128]{4,3,2,1,0:T(8,128)S(1)}, u32[]{:S(2)}, u32[]{:S(2)}) collective-permute-start(f32[2,2,1,128,128]{4,3,2,1,0:T(8,128)S(1)} %get-tuple-element.37), channel_id=1, source_target_pairs={{1,0},{2,1},{3,2},{4,3},{5,4},{6,5},{7,6},{8,7},{9,8},{10,9},{11,1... | collective-permute-start | bytes 786440 | tf_op jit(solution)/shard_map/ppermute | solution.py:22
  81.6 2.0 %collective-permute-done.12 = f32[2,2,1,128,128]{4,3,2,1,0:T(8,128)S(1)} collective-permute-done((f32[2,2,1,128,128]{4,3,2,1,0:T(8,128)S(1)}, f32[2,2,1,128,128]{4,3,2,1,0:T(8,128)S(1)}, u32[]{:S(2)}, u32[]{:S(2)}) %collective-permute-start.12) | collective-permute-done | bytes 262176 | tf_op jit(solution)/shard_map/ppermute | solution.py:22
  84.4 0.7 fusion.51
  85.1 18.0 %reduce-scatter.2.cloned.1.call-done = f32[2,2,64,128]{3,2,1,0:T(8,128)} async-done(((f32[2,2,128,128]{3,2,1,0:T(8,128)}), f32[2,2,64,128]{3,2,1,0:T(8,128)}) %reduce-scatter.2.cloned.1.call-update) | async-done | bytes 131088 | tf_op jit(solution)/shard_map/reduce_scatter | solution.py:91
  (72 shorter events, 8.6 us)
Async XLA Ops:
  6.5 4.5 %copy-start.4 = (f32[1,2]{1,0:T(1,128)S(1)}, f32[1,2]{1,0:T(1,128)}, u32[]{:S(2)}) copy-start(f32[1,2]{1,0:T(1,128)} %param.8) | copy-start | bytes 28
  6.5 5.2 %copy-start.1 = (f32[2,128,128]{2,1,0:T(8,128)S(1)}, f32[2,128,128]{2,1,0:T(8,128)}, u32[]{:S(2)}) copy-start(f32[2,128,128]{2,1,0:T(8,128)} %param.7) | copy-start | bytes 393220
  6.5 96.6 %reduce-scatter.2.cloned.1.call-start = ((), (), s32[]{:S(2)}) async-start(), calls=%async_computation.1 | async-start | bytes 393216 | tf_op jit(solution)/shard_map/reduce_scatter | solution.py:91
  6.6 8.2 %collective-permute-start = (f32[2,2,1,128,128]{4,3,2,1,0:T(8,128)S(1)}, f32[2,2,1,128,128]{4,3,2,1,0:T(8,128)S(1)}, u32[]{:S(2)}, u32[]{:S(2)}) collective-permute-start(f32[2,2,1,128,128]{4,3,2,1,0:T(8,128)S(1)} %broadcast.166), channel_id=1, source_target_pairs={{1,0},{2,1},{3,2},{4,3},{5,4},{6,5},{7,6},{8,7},{9,8},{10,9},{11,1... | collective-permute-start | bytes 786440 | tf_op jit(solution)/shard_map/ppermute | solution.py:22
  8.0 6.8 %collective-permute-start.1 = (f32[2,2,1,128,128]{4,3,2,1,0:T(8,128)S(1)}, f32[2,2,1,128,128]{4,3,2,1,0:T(8,128)S(1)}, u32[]{:S(2)}, u32[]{:S(2)}) collective-permute-start(f32[2,2,1,128,128]{4,3,2,1,0:T(8,128)S(1)} %broadcast.166), channel_id=1, source_target_pairs={{0,1},{1,2},{2,3},{3,4},{4,5},{5,6},{6,7},{7,8},{8,9},{9,10},{10,1... | collective-permute-start | bytes 786440 | tf_op jit(solution)/shard_map/ppermute | solution.py:20
  12.4 1.0 copy-start.2
  13.3 1.3 %copy-start.3 = (s32[2,128,128]{2,1,0:T(8,128)S(1)}, s32[2,128,128]{2,1,0:T(8,128)}, u32[]{:S(2)}) copy-start(s32[2,128,128]{2,1,0:T(8,128)} %param.9) | copy-start | bytes 393220
  14.9 1.0 copy-start
  16.0 7.4 %collective-permute-start.3 = (f32[2,2,1,128,128]{4,3,2,1,0:T(8,128)S(1)}, f32[2,2,1,128,128]{4,3,2,1,0:T(8,128)S(1)}, u32[]{:S(2)}, u32[]{:S(2)}) collective-permute-start(f32[2,2,1,128,128]{4,3,2,1,0:T(8,128)S(1)} %get-tuple-element.68), channel_id=1, source_target_pairs={{0,1},{1,2},{2,3},{3,4},{4,5},{5,6},{6,7},{7,8},{8,9},{9,10},{10,1... | collective-permute-start | bytes 786440 | tf_op jit(solution)/shard_map/ppermute | solution.py:20
  21.8 5.4 %collective-permute-start.2 = (f32[2,2,1,128,128]{4,3,2,1,0:T(8,128)S(1)}, f32[2,2,1,128,128]{4,3,2,1,0:T(8,128)S(1)}, u32[]{:S(2)}, u32[]{:S(2)}) collective-permute-start(f32[2,2,1,128,128]{4,3,2,1,0:T(8,128)S(1)} %get-tuple-element.67), channel_id=1, source_target_pairs={{1,0},{2,1},{3,2},{4,3},{5,4},{6,5},{7,6},{8,7},{9,8},{10,9},{11,1... | collective-permute-start | bytes 786440 | tf_op jit(solution)/shard_map/ppermute | solution.py:22
  28.1 8.1 %collective-permute-start.5 = (f32[2,2,1,128,128]{4,3,2,1,0:T(8,128)S(1)}, f32[2,2,1,128,128]{4,3,2,1,0:T(8,128)S(1)}, u32[]{:S(2)}, u32[]{:S(2)}) collective-permute-start(f32[2,2,1,128,128]{4,3,2,1,0:T(8,128)S(1)} %get-tuple-element.62), channel_id=1, source_target_pairs={{0,1},{1,2},{2,3},{3,4},{4,5},{5,6},{6,7},{7,8},{8,9},{9,10},{10,1... | collective-permute-start | bytes 786440 | tf_op jit(solution)/shard_map/ppermute | solution.py:20
  34.8 3.4 %collective-permute-start.4 = (f32[2,2,1,128,128]{4,3,2,1,0:T(8,128)S(1)}, f32[2,2,1,128,128]{4,3,2,1,0:T(8,128)S(1)}, u32[]{:S(2)}, u32[]{:S(2)}) collective-permute-start(f32[2,2,1,128,128]{4,3,2,1,0:T(8,128)S(1)} %get-tuple-element.61), channel_id=1, source_target_pairs={{1,0},{2,1},{3,2},{4,3},{5,4},{6,5},{7,6},{8,7},{9,8},{10,9},{11,1... | collective-permute-start | bytes 786440 | tf_op jit(solution)/shard_map/ppermute | solution.py:22
  39.1 8.3 %collective-permute-start.7 = (f32[2,2,1,128,128]{4,3,2,1,0:T(8,128)S(1)}, f32[2,2,1,128,128]{4,3,2,1,0:T(8,128)S(1)}, u32[]{:S(2)}, u32[]{:S(2)}) collective-permute-start(f32[2,2,1,128,128]{4,3,2,1,0:T(8,128)S(1)} %get-tuple-element.56), channel_id=1, source_target_pairs={{0,1},{1,2},{2,3},{3,4},{4,5},{5,6},{6,7},{7,8},{8,9},{9,10},{10,1... | collective-permute-start | bytes 786440 | tf_op jit(solution)/shard_map/ppermute | solution.py:20
  46.1 3.4 %collective-permute-start.6 = (f32[2,2,1,128,128]{4,3,2,1,0:T(8,128)S(1)}, f32[2,2,1,128,128]{4,3,2,1,0:T(8,128)S(1)}, u32[]{:S(2)}, u32[]{:S(2)}) collective-permute-start(f32[2,2,1,128,128]{4,3,2,1,0:T(8,128)S(1)} %get-tuple-element.55), channel_id=1, source_target_pairs={{1,0},{2,1},{3,2},{4,3},{5,4},{6,5},{7,6},{8,7},{9,8},{10,9},{11,1... | collective-permute-start | bytes 786440 | tf_op jit(solution)/shard_map/ppermute | solution.py:22
  50.3 8.7 %collective-permute-start.9 = (f32[2,2,1,128,128]{4,3,2,1,0:T(8,128)S(1)}, f32[2,2,1,128,128]{4,3,2,1,0:T(8,128)S(1)}, u32[]{:S(2)}, u32[]{:S(2)}) collective-permute-start(f32[2,2,1,128,128]{4,3,2,1,0:T(8,128)S(1)} %get-tuple-element.50), channel_id=1, source_target_pairs={{0,1},{1,2},{2,3},{3,4},{4,5},{5,6},{6,7},{7,8},{8,9},{9,10},{10,1... | collective-permute-start | bytes 786440 | tf_op jit(solution)/shard_map/ppermute | solution.py:20
  57.4 3.4 %collective-permute-start.8 = (f32[2,2,1,128,128]{4,3,2,1,0:T(8,128)S(1)}, f32[2,2,1,128,128]{4,3,2,1,0:T(8,128)S(1)}, u32[]{:S(2)}, u32[]{:S(2)}) collective-permute-start(f32[2,2,1,128,128]{4,3,2,1,0:T(8,128)S(1)} %get-tuple-element.49), channel_id=1, source_target_pairs={{1,0},{2,1},{3,2},{4,3},{5,4},{6,5},{7,6},{8,7},{9,8},{10,9},{11,1... | collective-permute-start | bytes 786440 | tf_op jit(solution)/shard_map/ppermute | solution.py:22
  61.7 8.5 %collective-permute-start.11 = (f32[2,2,1,128,128]{4,3,2,1,0:T(8,128)S(1)}, f32[2,2,1,128,128]{4,3,2,1,0:T(8,128)S(1)}, u32[]{:S(2)}, u32[]{:S(2)}) collective-permute-start(f32[2,2,1,128,128]{4,3,2,1,0:T(8,128)S(1)} %get-tuple-element.44), channel_id=1, source_target_pairs={{0,1},{1,2},{2,3},{3,4},{4,5},{5,6},{6,7},{7,8},{8,9},{9,10},{10,1... | collective-permute-start | bytes 786440 | tf_op jit(solution)/shard_map/ppermute | solution.py:20
  68.8 3.4 %collective-permute-start.10 = (f32[2,2,1,128,128]{4,3,2,1,0:T(8,128)S(1)}, f32[2,2,1,128,128]{4,3,2,1,0:T(8,128)S(1)}, u32[]{:S(2)}, u32[]{:S(2)}) collective-permute-start(f32[2,2,1,128,128]{4,3,2,1,0:T(8,128)S(1)} %get-tuple-element.43), channel_id=1, source_target_pairs={{1,0},{2,1},{3,2},{4,3},{5,4},{6,5},{7,6},{8,7},{9,8},{10,9},{11,1... | collective-permute-start | bytes 786440 | tf_op jit(solution)/shard_map/ppermute | solution.py:22
  73.2 8.5 %collective-permute-start.13 = (f32[2,2,1,128,128]{4,3,2,1,0:T(8,128)S(1)}, f32[2,2,1,128,128]{4,3,2,1,0:T(8,128)S(1)}, u32[]{:S(2)}, u32[]{:S(2)}) collective-permute-start(f32[2,2,1,128,128]{4,3,2,1,0:T(8,128)S(1)} %get-tuple-element.38), channel_id=1, source_target_pairs={{0,1},{1,2},{2,3},{3,4},{4,5},{5,6},{6,7},{7,8},{8,9},{9,10},{10,1... | collective-permute-start | bytes 786440 | tf_op jit(solution)/shard_map/ppermute | solution.py:20
  80.2 3.4 %collective-permute-start.12 = (f32[2,2,1,128,128]{4,3,2,1,0:T(8,128)S(1)}, f32[2,2,1,128,128]{4,3,2,1,0:T(8,128)S(1)}, u32[]{:S(2)}, u32[]{:S(2)}) collective-permute-start(f32[2,2,1,128,128]{4,3,2,1,0:T(8,128)S(1)} %get-tuple-element.37), channel_id=1, source_target_pairs={{1,0},{2,1},{3,2},{4,3},{5,4},{6,5},{7,6},{8,7},{9,8},{10,9},{11,1... | collective-permute-start | bytes 786440 | tf_op jit(solution)/shard_map/ppermute | solution.py:22
Sparse Core Ops, SparseCore 0:
  85.3 17.8 reduce-scatter.1
where the time goes:
time: 111 us; the launch traced here: 110 us
  starting transfers between devices  52.9 us (48%)
  waiting for transfers between devices  31.8 us (29%)
  between operations  13.9 us (13%)
  other arithmetic  8.48 us (8%)
  local copies, waits for them, and re-layouts  2.92 us (3%)
    ppermute x7, starting transfers between devices, padded(): lax.ppermute(tail, axis, [(i, (i + 1) % count) for i in range(ends)])  43.7 us
    reduce_scatter x1, waiting for transfers between devices, per_device(): return lax.psum_scatter(terms, 'freq', scatter_dimension=2, tiled=True)  18 us
    ppermute x7, waiting for transfers between devices, padded(): lax.ppermute(head, axis, [((i + 1) % count, i) for i in range(ends)])  13.8 us
    ppermute x7, starting transfers between devices, padded(): lax.ppermute(head, axis, [((i + 1) % count, i) for i in range(ends)])  9.18 us
    add x7, other arithmetic, neighbours(): beside_all + jnp.pad(center[:, :, :, :, 1:], pad_z_low)  2.47 us
  transfers between devices with their start and end apart: 15, of which 7 were waited for; matrix products, arithmetic and copies ran while one was open for 4% of the time, Pallas kernels for 0%

commit v1 on v0

v1 whole, which is shorter than its diff:
```python
import functools

import jax
import jax.numpy as jnp
from jax import lax
from jax.experimental import pallas as pl
from jax.experimental.pallas import tpu as pltpu
from jax.sharding import PartitionSpec as P

STEPS = 4
OMEGA_RELAX = 0.8
MESH = pl.DeviceIdType.MESH

PAIRS = 2
MARGIN = 8


def spread(values):
    rows, lanes = values.shape
    row = lax.broadcasted_iota(jnp.int32, values.shape, 0)
    lane = lax.broadcasted_iota(jnp.int32, values.shape, 1)
    zero = jnp.zeros_like(values)
    up = jnp.where(row == 0, zero, pltpu.roll(values, 1, 0))
    down = jnp.where(row == rows - 1, zero, pltpu.roll(values, rows - 1, 0))
    left = jnp.where(lane == 0, zero, pltpu.roll(values, 1, 1))
    right = jnp.where(lane == lanes - 1, zero, pltpu.roll(values, lanes - 1, 1))
    return (up + down) + (left + right)


def kernel(
    freqs, spaces, rows_all, shifts_ref, probes_ref, back_ref, medium_ref, receivers_ref, out_ref,
    probes_in, back_in, medium_in, listen_in, shift_out, shift_in,
    inverse, fields, halos, terms,
    send_in, recv_probes, recv_medium, recv_listen, recv_back, send_back,
    send_shift, recv_shift, send_halo, recv_halo, send_out, recv_out,
):
    own = probes_ref.shape[1]
    layers = PAIRS * own
    num_probes = probes_ref.shape[0]
    window = probes_in.shape[2]
    part = window - 2 * MARGIN
    h = lax.axis_index("freq")
    s = lax.axis_index("space")
    group = s // (2 * PAIRS)
    base = group * (2 * PAIRS)
    q = (s // 2) % PAIRS
    c = s % 2
    has_low = jnp.logical_or(c != 0, group != 0)
    has_high = jnp.logical_or(c != 1, group != spaces // (2 * PAIRS) - 1)
    low = jnp.where(c == 0, s - 3, s - 1)
    high = jnp.where(c == 0, s + 1, s + 3)

    barrier = pltpu.get_barrier_semaphore()
    for f in range(freqs):
        for member in range(2 * PAIRS):
            @pl.when(jnp.logical_not(jnp.logical_and(h == f, base + member == s)))
            def _():
                pl.semaphore_signal(barrier, inc=1, device_id=(f, base + member), device_id_type=MESH)

    @pl.when(jnp.logical_and(has_low, c == 0))
    def _():
        pl.semaphore_signal(barrier, inc=1, device_id=(h, low), device_id_type=MESH)

    @pl.when(jnp.logical_and(has_high, c == 1))
    def _():
        pl.semaphore_signal(barrier, inc=1, device_id=(h, high), device_id_type=MESH)

    pick = lax.broadcasted_iota(jnp.int32, shift_out.shape, 0)
    shift_out[...] = jnp.where(pick == 0, shifts_ref[0, 0], shifts_ref[0, 1])

    @pl.when(jnp.logical_not(has_low))
    def _():
        halos[:, 0] = jnp.zeros_like(halos[:, 0])

    @pl.when(jnp.logical_not(has_high))
    def _():
        halos[:, 1] = jnp.zeros_like(halos[:, 1])

    outside = jnp.logical_or(
        jnp.logical_and(has_low, c == 0), jnp.logical_and(has_high, c == 1)
    )
    pl.semaphore_wait(barrier, 2 * PAIRS * freqs - 1 + outside.astype(jnp.int32))

    def first_row(f, pair):
        start = jnp.clip((f * PAIRS + pair) * part - MARGIN, 0, rows_all - window)
        return pl.multiple_of(start, 8)

    def put(src, dst, send_sem, recv_sem, f, to, go):
        here = jnp.logical_and(h == f, s == to)

        @pl.when(jnp.logical_not(here))
        def _():
            copy = pltpu.make_async_remote_copy(
                src_ref=src, dst_ref=dst, send_sem=send_sem, recv_sem=recv_sem,
                device_id=(f, to), device_id_type=MESH,
            )
            if go:
                copy.start()
            else:
                copy.wait_send()

        if go:
            @pl.when(here)
            def _():
                pltpu.make_async_copy(src, dst, recv_sem).start()

    def arrived(dst, sem):
        pltpu.make_async_copy(dst, dst, sem).wait()

    mine = pl.ds(c * own, own)

    def send_inputs(go):
        for f in range(freqs):
            @pl.when(h != f)
            def _():
                copy = pltpu.make_async_remote_copy(
                    src_ref=shift_out, dst_ref=shift_in.at[h], send_sem=send_shift.at[f],
                    recv_sem=recv_shift.at[h], device_id=(f, s), device_id_type=MESH,
                )
                if go:
                    copy.start()
                else:
                    copy.wait_send()

        for pair in range(PAIRS):
            to = base + 2 * pair + q
            rows = pl.ds(first_row(h, pair), window)
            put(medium_ref.at[:, rows], medium_in.at[mine],
                send_in.at[0, pair], recv_medium.at[c], h, to, go)
            put(probes_ref.at[:, :, rows], probes_in.at[:, mine],
                send_in.at[1, pair], recv_probes.at[c], h, to, go)
        for f in range(freqs):
            for pair in range(PAIRS):
                to = base + 2 * pair + q
                rows = pl.ds(first_row(f, pair), window)
                put(back_ref.at[0, :, :, rows], back_in.at[h, :, mine],
                    send_back.at[f, pair], recv_back.at[h, c], f, to, go)
        for pair in range(PAIRS):
            to = base + 2 * pair + q
            rows = pl.ds(first_row(h, pair), window)
            put(receivers_ref.at[:, rows], listen_in.at[mine],
                send_in.at[2, pair], recv_listen.at[c], h, to, go)

    send_inputs(True)

    shift_in[h] = shift_out[...]

    def halo(k, block, side, go):
        there = has_low if side == 0 else has_high
        layer = 0 if side == 0 else layers - 1

        @pl.when(there)
        def _():
            copy = pltpu.make_async_remote_copy(
                src_ref=fields.at[k, layer, block],
                dst_ref=halos.at[k, 1 - side, block],
                send_sem=send_halo.at[k, side, block],
                recv_sem=recv_halo.at[k, 1 - side, block],
                device_id=(h, low if side == 0 else high), device_id_type=MESH,
            )
            if go:
                copy.start()
            else:
                copy.wait_send()

    def halo_arrived(k, block, side):
        there = has_low if side == 0 else has_high

        @pl.when(there)
        def _():
            arrived(halos.at[k, side, block], recv_halo.at[k, side, block])

    def scaled(f, layer):
        shift_re, shift_im = shift_in[f, 0:1], shift_in[f, 1:2]
        back_re, back_im = back_in[f, 0, layer], back_in[f, 1, layer]
        return shift_re * back_re - shift_im * back_im, shift_re * back_im + shift_im * back_re

    edges = (0, layers - 1)
    inner = tuple(range(1, layers - 1))

    for owner in range(2):
        arrived(medium_in.at[pl.ds(owner * own, own)], recv_medium.at[owner])
        arrived(probes_in.at[:, pl.ds(owner * own, own)], recv_probes.at[owner])

    def first(f, layer):
        shift_re, shift_im = shift_in[f, 0:1], shift_in[f, 1:2]
        medium = medium_in[layer]
        diag_re = 6.0 + shift_re * medium
        diag_im = shift_im * medium
        scale = OMEGA_RELAX / (diag_re * diag_re + diag_im * diag_im)
        inv_re = diag_re * scale
        inv_im = -diag_im * scale
        inverse[f, 0, layer] = inv_re
        inverse[f, 1, layer] = inv_im
        scaled_re, scaled_im = scaled(f, layer)
        start_re = inv_re * scaled_re - inv_im * scaled_im
        start_im = inv_re * scaled_im + inv_im * scaled_re
        for p in range(num_probes):
            probe = probes_in[p, layer]
            fields[0, layer, f * num_probes + p, 0] = start_re * probe
            fields[0, layer, f * num_probes + p, 1] = start_im * probe

    @pl.loop(0, freqs)
    def _(turn):
        f = lax.rem(h + turn, freqs)

        @pl.when(turn != 0)
        def _():
            arrived(shift_in.at[f], recv_shift.at[f])

        for owner in range(2):
            arrived(back_in.at[f, :, pl.ds(owner * own, own)], recv_back.at[f, owner])
        for side, layer in enumerate(edges):
            first(f, layer)
            for p in range(num_probes):
                halo(0, f * num_probes + p, side, True)
        for layer in inner:
            first(f, layer)

    def update(k, f, block, layer, sign):
        new = []
        for part_of in range(2):
            below = halos[k, 0, block, part_of] if layer == 0 else fields[k, layer - 1, block, part_of]
            above = halos[k, 1, block, part_of] if layer == layers - 1 else fields[k, layer + 1, block, part_of]
            new.append((below + above) + spread(fields[k, layer, block, part_of]))
        sum_re, sum_im = new
        inv_re = inverse[f, 0, layer]
        inv_im = sign * inverse[f, 1, layer]
        origin = 0 if k < STEPS - 1 else STEPS - 1
        keep = 1.0 - OMEGA_RELAX
        next_re = keep * fields[k, layer, block, 0] + fields[origin, layer, block, 0]
        next_im = keep * fields[k, layer, block, 1] + fields[origin, layer, block, 1]
        next_re = next_re + (inv_re * sum_re - inv_im * sum_im)
        next_im = next_im + (inv_re * sum_im + inv_im * sum_re)
        return next_re, next_im

    last = 2 * (STEPS - 1) - 1
    for k in range(last + 1):
        if k == STEPS - 2:
            for owner in range(2):
                arrived(listen_in.at[pl.ds(owner * own, own)], recv_listen.at[owner])
        sign = 1.0 if k < STEPS - 1 else -1.0

        def advance(f, block, layer, k=k, sign=sign):
            next_re, next_im = update(k, f, block, layer, sign)
            if k == STEPS - 2:
                listen = listen_in[layer].astype(jnp.float32)
                next_re = next_re * listen
                next_im = next_im * listen
                inv_re, inv_im = inverse[f, 0, layer], inverse[f, 1, layer]
                next_re, next_im = (
                    inv_re * next_re + inv_im * next_im,
                    inv_re * next_im - inv_im * next_re,
                )
            fields[k + 1, layer, block, 0] = next_re
            fields[k + 1, layer, block, 1] = next_im

        if k < last:
            @pl.loop(0, freqs)
            def _(turn):
                f = lax.rem(h + turn, freqs)
                for p in range(num_probes):
                    block = f * num_probes + p
                    for side, layer in enumerate(edges):
                        halo_arrived(k, block, side)
                        advance(f, block, layer)
                        halo(k + 1, block, side, True)

            @pl.loop(0, freqs)
            def _(f):
                for p in range(num_probes):
                    for layer in inner:
                        advance(f, f * num_probes + p, layer)

    def add_terms(f, layers_of, start):
        for layer in layers_of:
            scaled_re, scaled_im = scaled(f, layer)
            for p in range(num_probes):
                next_re, next_im = update(last, f, f * num_probes + p, layer, -1.0)
                term = scaled_re * next_re + scaled_im * next_im
                terms[p, layer] = term if start else terms[p, layer] + term

    add_terms(0, inner, True)

    @pl.loop(1, freqs)
    def _(f):
        add_terms(f, inner, False)

    for block in range(num_probes):
        halo_arrived(last, block, 0)
        halo_arrived(last, block, 1)
    add_terms(0, edges, True)

    @pl.loop(1, freqs)
    def _(f):
        for p in range(num_probes):
            halo_arrived(last, f * num_probes + p, 0)
            halo_arrived(last, f * num_probes + p, 1)
        add_terms(f, edges, False)

    inside = pl.multiple_of((h * PAIRS + q) * part - first_row(h, q), 8)

    def send_terms(go):
        for owner in range(2):
            put(terms.at[:, pl.ds(owner * own, own), pl.ds(inside, part)],
                out_ref.at[:, :, pl.ds(pl.multiple_of(q * part, 8), part)],
                send_out.at[owner], recv_out.at[q], h, base + 2 * c + owner, go)

    send_terms(True)
    for pair in range(PAIRS):
        arrived(out_ref.at[:, :, pl.ds(pair * part, part)], recv_out.at[pair])
    send_terms(False)
    send_inputs(False)

    @pl.loop(0, last + 1)
    def _(k):
        @pl.loop(0, freqs * num_probes)
        def _(block):
            halo(k, block, 0, False)
            halo(k, block, 1, False)


def per_device(freqs, spaces, probes, background, medium, shifts, receivers):
    num_probes, own, rows_all, lanes = probes.shape
    layers = PAIRS * own
    part = rows_all // (freqs * PAIRS)
    window = part + 2 * MARGIN
    blocks = freqs * num_probes
    count = 2 * (STEPS - 1)
    dma = pltpu.SemaphoreType.DMA
    any_spec = pl.BlockSpec(memory_space=pl.ANY)
    return pl.pallas_call(
        functools.partial(kernel, freqs, spaces, rows_all),
        out_shape=jax.ShapeDtypeStruct((num_probes, own, rows_all // freqs, lanes), jnp.float32),
        in_specs=[pl.BlockSpec(memory_space=pltpu.SMEM)] + [any_spec] * 4,
        out_specs=any_spec,
        scratch_shapes=[
            pltpu.VMEM((num_probes, layers, window, lanes), jnp.float32),
            pltpu.VMEM((freqs, 2, layers, window, lanes), jnp.float32),
            pltpu.VMEM((layers, window, lanes), jnp.float32),
            pltpu.VMEM((layers, window, lanes), jnp.int32),
            pltpu.VMEM((8, lanes), jnp.float32),
            pltpu.VMEM((freqs, 8, lanes), jnp.float32),
            pltpu.VMEM((freqs, 2, layers, window, lanes), jnp.float32),
            pltpu.VMEM((count, layers, blocks, 2, window, lanes), jnp.float32),
            pltpu.VMEM((count, 2, blocks, 2, window, lanes), jnp.float32),
            pltpu.VMEM((num_probes, layers, window, lanes), jnp.float32),
            dma((3, PAIRS)),
            dma((2,)),
            dma((2,)),
            dma((2,)),
            dma((freqs, 2)),
            dma((freqs, PAIRS)),
            dma((freqs,)),
            dma((freqs,)),
            dma((count, 2, blocks)),
            dma((count, 2, blocks)),
            dma((2,)),
            dma((PAIRS,)),
        ],
        compiler_params=pltpu.CompilerParams(collective_id=0, has_side_effects=True),
    )(shifts, probes, background, medium, receivers)


def solution(mesh):
    in_specs = (
        P(None, "space", None, None),
        P("freq", None, "space", None, None),
        P("space", None, None),
        P("freq", None),
        P("space", None, None),
    )
    out_specs = P(None, "space", "freq", None)
    return jax.shard_map(
        functools.partial(per_device, mesh.shape["freq"], mesh.shape["space"]),
        mesh=mesh, in_specs=in_specs, out_specs=out_specs, check_vma=False,
    )
```

time: 111 us -> 38.8 us (0.35)
  the two profiles are of different devices: /device:TPU:0 before, /device:TPU:21 now
where the time goes in v1:
time: 38.8 us; the launch traced here: 38.6 us
  Pallas kernels  37 us (95%)
  local copies, waits for them, and re-layouts  1.57 us (4%)
    pallas_call x1, Pallas kernels, per_device(): pl.pallas_call(functools.partial(kernel, freqs, spaces, rows_all), out_sh...  37 us
    unnamed x1, local copies, waits for them, and re-layouts  1.57 us

profile of v1, /device:TPU:21, one launch (start us, length us, event | category | flops | bytes accessed | tf_op | source)
XLA Modules:
  0.0 38.6 jit_solution(15333442622350167081)
XLA Ops:
  0.0 37.0 %shard_map.55 = f32[2,2,64,128]{3,2,1,0:T(8,128)} custom-call(f32[1,2]{1,0:T(1,128)} %shifts_ref.1, f32[2,2,128,128]{3,2,1,0:T(8,128)} %probes_ref.1, f32[1,2,2,128,128]{4,3,2,1,0:T(8,128)} %back_ref.1, f32[2,128,128]{2,1,0:T(8,128)} %medium_ref.1, s32[2,128,128]{2,1,0:T(8,128)} %receivers_ref.1), custom_call_target="tpu_custom_call" | custom-call | tf_op jit(solution)/shard_map/pallas_call | solution.py:332
  37.0 1.6 %copy.7 = f32[2,2,64,128]{3,2,1,0:T(8,128)} copy(f32[2,2,64,128]{3,2,1,0:T(8,128)} %shard_map.55) | data formatting | bytes 262144

commit v2 on v1

v2 whole, which is shorter than its diff:
```python
import functools

import jax
import jax.numpy as jnp
from jax import lax
from jax.experimental import pallas as pl
from jax.experimental.pallas import tpu as pltpu
from jax.sharding import PartitionSpec as P

STEPS = 4
OMEGA_RELAX = 0.8
MESH = pl.DeviceIdType.MESH

PAIRS = 2
MARGIN = 8
DEPTH = 2


def spread(values):
    rows, lanes = values.shape
    row = lax.broadcasted_iota(jnp.int32, values.shape, 0)
    lane = lax.broadcasted_iota(jnp.int32, values.shape, 1)
    zero = jnp.zeros_like(values)
    up = jnp.where(row == 0, zero, pltpu.roll(values, 1, 0))
    down = jnp.where(row == rows - 1, zero, pltpu.roll(values, rows - 1, 0))
    left = jnp.where(lane == 0, zero, pltpu.roll(values, 1, 1))
    right = jnp.where(lane == lanes - 1, zero, pltpu.roll(values, lanes - 1, 1))
    return (up + down) + (left + right)


def kernel(
    freqs, spaces, rows_all, shifts_ref, probes_ref, back_ref, medium_ref, receivers_ref, out_ref,
    probes_in, back_in, medium_in, listen_in, shift_out, shift_in,
    inverse, fields, terms,
    send_in, recv_probes, recv_medium, recv_listen, recv_back, send_back,
    send_shift, recv_shift, send_halo, recv_halo, send_near, recv_near, send_out, recv_out,
):
    own = probes_ref.shape[1]
    layers = PAIRS * own
    num_probes = probes_ref.shape[0]
    window = probes_in.shape[2]
    part = window - 2 * MARGIN
    last = 2 * (STEPS - 1) - 1
    sent = tuple(range(0, last, DEPTH))
    h = lax.axis_index("freq")
    s = lax.axis_index("space")
    group = s // (2 * PAIRS)
    base = group * (2 * PAIRS)
    q = (s // 2) % PAIRS
    c = s % 2
    has_low = jnp.logical_or(c != 0, group != 0)
    has_high = jnp.logical_or(c != 1, group != spaces // (2 * PAIRS) - 1)
    low = jnp.where(c == 0, s - 3, s - 1)
    high = jnp.where(c == 0, s + 1, s + 3)

    barrier = pltpu.get_barrier_semaphore()
    for f in range(freqs):
        for member in range(2 * PAIRS):
            @pl.when(jnp.logical_not(jnp.logical_and(h == f, base + member == s)))
            def _():
                pl.semaphore_signal(barrier, inc=1, device_id=(f, base + member), device_id_type=MESH)

    @pl.when(jnp.logical_and(has_low, c == 0))
    def _():
        pl.semaphore_signal(barrier, inc=1, device_id=(h, low), device_id_type=MESH)

    @pl.when(jnp.logical_and(has_high, c == 1))
    def _():
        pl.semaphore_signal(barrier, inc=1, device_id=(h, high), device_id_type=MESH)

    pick = lax.broadcasted_iota(jnp.int32, shift_out.shape, 0)
    shift_out[...] = jnp.where(pick == 0, shifts_ref[0, 0], shifts_ref[0, 1])

    @pl.when(jnp.logical_not(has_low))
    def _():
        for k in sent:
            fields[k, 0:DEPTH] = jnp.zeros_like(fields[k, 0:DEPTH])
        listen_in[0] = jnp.zeros_like(listen_in[0])

    @pl.when(jnp.logical_not(has_high))
    def _():
        for k in sent:
            fields[k, layers + DEPTH :] = jnp.zeros_like(fields[k, layers + DEPTH :])
        listen_in[layers + 1] = jnp.zeros_like(listen_in[layers + 1])

    outside = jnp.logical_or(
        jnp.logical_and(has_low, c == 0), jnp.logical_and(has_high, c == 1)
    )
    pl.semaphore_wait(barrier, 2 * PAIRS * freqs - 1 + outside.astype(jnp.int32))

    def first_row(f, pair):
        start = jnp.clip((f * PAIRS + pair) * part - MARGIN, 0, rows_all - window)
        return pl.multiple_of(start, 8)

    def put(src, dst, send_sem, recv_sem, f, to, go):
        here = jnp.logical_and(h == f, s == to)

        @pl.when(jnp.logical_not(here))
        def _():
            copy = pltpu.make_async_remote_copy(
                src_ref=src, dst_ref=dst, send_sem=send_sem, recv_sem=recv_sem,
                device_id=(f, to), device_id_type=MESH,
            )
            if go:
                copy.start()
            else:
                copy.wait_send()

        if go:
            @pl.when(here)
            def _():
                pltpu.make_async_copy(src, dst, recv_sem).start()

    def arrived(dst, sem):
        pltpu.make_async_copy(dst, dst, sem).wait()

    mine = pl.ds(c * own, own)
    mine_near = pl.ds(1 + c * own, own)

    def send_inputs(go):
        for f in range(freqs):
            @pl.when(h != f)
            def _():
                copy = pltpu.make_async_remote_copy(
                    src_ref=shift_out, dst_ref=shift_in.at[h], send_sem=send_shift.at[f],
                    recv_sem=recv_shift.at[h], device_id=(f, s), device_id_type=MESH,
                )
                if go:
                    copy.start()
                else:
                    copy.wait_send()

        def back(f):
            for step in range(PAIRS):
                pair = lax.rem(q + 1 + step, PAIRS)
                rows = pl.ds(first_row(f, pair), window)
                put(back_ref.at[0, :, :, rows], back_in.at[h, :, mine],
                    send_back.at[f, pair], recv_back.at[h, c], f, base + 2 * pair + q, go)

        def shared(index, src, dst, sem):
            for step in range(PAIRS):
                pair = lax.rem(q + 1 + step, PAIRS)
                rows = pl.ds(first_row(h, pair), window)
                put(src(rows), dst, send_in.at[index, pair], sem.at[c], h, base + 2 * pair + q, go)

        shared(0, lambda rows: medium_ref.at[:, rows], medium_in.at[mine_near], recv_medium)
        back(h)
        shared(1, lambda rows: probes_ref.at[:, :, rows], probes_in.at[:, mine], recv_probes)
        for turn in range(1, freqs):
            back(lax.rem(h + turn, freqs))
        shared(2, lambda rows: receivers_ref.at[:, rows], listen_in.at[mine_near], recv_listen)

    send_inputs(True)

    shift_in[h] = shift_out[...]

    def send(src, dst, send_sem, recv_sem, side, go):
        @pl.when(has_low if side == 0 else has_high)
        def _():
            copy = pltpu.make_async_remote_copy(
                src_ref=src, dst_ref=dst, send_sem=send_sem, recv_sem=recv_sem,
                device_id=(h, low if side == 0 else high), device_id_type=MESH,
            )
            if go:
                copy.start()
            else:
                copy.wait_send()

    def halo(k, block, side, go):
        src = pl.ds(DEPTH if side == 0 else layers, DEPTH)
        dst = pl.ds(layers + DEPTH if side == 0 else 0, DEPTH)
        send(fields.at[k, src, block], fields.at[k, dst, block],
             send_halo.at[k // DEPTH, side, block], recv_halo.at[k // DEPTH, 1 - side, block], side, go)

    def halo_arrived(k, block):
        for side in range(2):
            @pl.when(has_low if side == 0 else has_high)
            def _():
                where = pl.ds(0 if side == 0 else layers + DEPTH, DEPTH)
                arrived(fields.at[k, where, block], recv_halo.at[k // DEPTH, side, block])

    def near(ref, index, side, go):
        send(ref.at[1 if side == 0 else layers], ref.at[layers + 1 if side == 0 else 0],
             send_near.at[index, side], recv_near.at[index, 1 - side], side, go)

    def near_arrived(ref, index):
        for side in range(2):
            @pl.when(has_low if side == 0 else has_high)
            def _():
                arrived(ref.at[0 if side == 0 else layers + 1], recv_near.at[index, side])

    def scaled(f, layer):
        shift_re, shift_im = shift_in[f, 0:1], shift_in[f, 1:2]
        back_re, back_im = back_in[f, 0, layer], back_in[f, 1, layer]
        return shift_re * back_re - shift_im * back_im, shift_re * back_im + shift_im * back_re

    def invert(f, index):
        shift_re, shift_im = shift_in[f, 0:1], shift_in[f, 1:2]
        medium = medium_in[index]
        diag_re = 6.0 + shift_re * medium
        diag_im = shift_im * medium
        scale = OMEGA_RELAX / (diag_re * diag_re + diag_im * diag_im)
        inv_re = diag_re * scale
        inv_im = -diag_im * scale
        inverse[f, 0, index] = inv_re
        inverse[f, 1, index] = inv_im
        return inv_re, inv_im

    order = list(range(DEPTH)) + [i for i in range(layers - DEPTH, layers) if i >= DEPTH]
    order += [i for i in range(layers) if i not in order]
    ready_low, ready_high = DEPTH, min(2 * DEPTH, layers)

    for owner in range(2):
        arrived(medium_in.at[pl.ds(1 + owner * own, own)], recv_medium.at[owner])
    for side in range(2):
        near(medium_in, 0, side, True)

    def first(turn):
        f = lax.rem(h + turn, freqs)

        @pl.when(turn != 0)
        def _():
            arrived(shift_in.at[f], recv_shift.at[f])

        for owner in range(2):
            arrived(back_in.at[f, :, pl.ds(owner * own, own)], recv_back.at[f, owner])

        @pl.when(turn == 0)
        def _():
            for owner in range(2):
                arrived(probes_in.at[:, pl.ds(owner * own, own)], recv_probes.at[owner])

        for done, layer in enumerate(order):
            inv_re, inv_im = invert(f, 1 + layer)
            scaled_re, scaled_im = scaled(f, layer)
            start_re = inv_re * scaled_re - inv_im * scaled_im
            start_im = inv_re * scaled_im + inv_im * scaled_re
            for p in range(num_probes):
                block = f * num_probes + p
                probe = probes_in[p, layer]
                fields[0, DEPTH + layer, block, 0] = start_re * probe
                fields[0, DEPTH + layer, block, 1] = start_im * probe
                if done + 1 == ready_low:
                    halo(0, block, 0, True)
                if done + 1 == ready_high:
                    halo(0, block, 1, True)

    pl.loop(0, freqs)(first)

    def update(k, f, block, at, sign):
        new = []
        for part_of in range(2):
            beside = fields[k, at - 1, block, part_of] + fields[k, at + 1, block, part_of]
            new.append(beside + spread(fields[k, at, block, part_of]))
        sum_re, sum_im = new
        inv_re = inverse[f, 0, at - 1]
        inv_im = sign * inverse[f, 1, at - 1]
        origin = 0 if k < STEPS - 1 else STEPS - 1
        keep = 1.0 - OMEGA_RELAX
        next_re = keep * fields[k, at, block, 0] + fields[origin, at, block, 0]
        next_im = keep * fields[k, at, block, 1] + fields[origin, at, block, 1]
        next_re = next_re + (inv_re * sum_re - inv_im * sum_im)
        next_im = next_im + (inv_re * sum_im + inv_im * sum_re)
        return next_re, next_im

    def advance(k, f, block, at):
        next_re, next_im = update(k, f, block, at, 1.0 if k < STEPS - 1 else -1.0)
        if k == STEPS - 2:
            listen = listen_in[at - 1].astype(jnp.float32)
            next_re = next_re * listen
            next_im = next_im * listen
            inv_re, inv_im = inverse[f, 0, at - 1], inverse[f, 1, at - 1]
            next_re, next_im = (
                inv_re * next_re + inv_im * next_im,
                inv_re * next_im - inv_im * next_re,
            )
        fields[k + 1, at, block, 0] = next_re
        fields[k + 1, at, block, 1] = next_im

    def invert_near(f):
        for side in range(2):
            there = has_low if side == 0 else has_high
            index = 0 if side == 0 else layers + 1

            @pl.when(there)
            def _():
                invert(f, index)

            @pl.when(jnp.logical_not(there))
            def _():
                inverse[f, :, index] = jnp.zeros_like(inverse[f, :, index])

    for k in sent[:-1]:
        if k == 0:
            near_arrived(medium_in, 0)
        if k == DEPTH:
            near_arrived(listen_in, 1)

        @pl.loop(0, freqs)
        def _(turn, k=k):
            f = lax.rem(h + turn, freqs)
            if k == 0:
                invert_near(f)
            for p in range(num_probes):
                block = f * num_probes + p
                halo_arrived(k, block)
                for at in range(1, layers + 3):
                    advance(k, f, block, at)
                for done, layer in enumerate(order):
                    advance(k + 1, f, block, DEPTH + layer)
                    if done + 1 == ready_low:
                        halo(k + DEPTH, block, 0, True)
                    if done + 1 == ready_high:
                        halo(k + DEPTH, block, 1, True)

        if k == 0:
            for owner in range(2):
                arrived(listen_in.at[pl.ds(1 + owner * own, own)], recv_listen.at[owner])
            for side in range(2):
                near(listen_in, 1, side, True)

    inside = pl.multiple_of((h * PAIRS + q) * part - first_row(h, q), 8)

    def send_terms(p, go):
        for owner in range(2):
            put(terms.at[p, pl.ds(owner * own, own), pl.ds(inside, part)],
                out_ref.at[p, :, pl.ds(pl.multiple_of(q * part, 8), part)],
                send_out.at[p, owner], recv_out.at[p, q], h, base + 2 * c + owner, go)

    def add_terms(f, p, start):
        block = f * num_probes + p
        halo_arrived(last - 1, block)
        for at in range(1, layers + 3):
            advance(last - 1, f, block, at)
        for layer in range(layers):
            scaled_re, scaled_im = scaled(f, layer)
            next_re, next_im = update(last, f, block, DEPTH + layer, -1.0)
            term = scaled_re * next_re + scaled_im * next_im
            terms[p, layer] = term if start else terms[p, layer] + term

    for p in range(num_probes):
        add_terms(h, p, True)

    if freqs > 2:
        @pl.loop(1, freqs - 1)
        def _(turn):
            for p in range(num_probes):
                add_terms(lax.rem(h + turn, freqs), p, False)

    for p in range(num_probes):
        if freqs > 1:
            add_terms(lax.rem(h + freqs - 1, freqs), p, False)
        send_terms(p, True)

    for p in range(num_probes):
        for pair in range(PAIRS):
            arrived(out_ref.at[p, :, pl.ds(pair * part, part)], recv_out.at[p, pair])
    for p in range(num_probes):
        send_terms(p, False)
    send_inputs(False)
    for side in range(2):
        near(medium_in, 0, side, False)
        near(listen_in, 1, side, False)
    for k in sent:
        @pl.loop(0, freqs * num_probes)
        def _(block, k=k):
            halo(k, block, 0, False)
            halo(k, block, 1, False)


def per_device(freqs, spaces, probes, background, medium, shifts, receivers):
    num_probes, own, rows_all, lanes = probes.shape
    layers = PAIRS * own
    part = rows_all // (freqs * PAIRS)
    window = part + 2 * MARGIN
    blocks = freqs * num_probes
    count = 2 * (STEPS - 1)
    dma = pltpu.SemaphoreType.DMA
    any_spec = pl.BlockSpec(memory_space=pl.ANY)
    return pl.pallas_call(
        functools.partial(kernel, freqs, spaces, rows_all),
        out_shape=jax.ShapeDtypeStruct((num_probes, own, rows_all // freqs, lanes), jnp.float32),
        in_specs=[pl.BlockSpec(memory_space=pltpu.SMEM)] + [any_spec] * 4,
        out_specs=any_spec,
        scratch_shapes=[
            pltpu.VMEM((num_probes, layers, window, lanes), jnp.float32),
            pltpu.VMEM((freqs, 2, layers, window, lanes), jnp.float32),
            pltpu.VMEM((layers + 2, window, lanes), jnp.float32),
            pltpu.VMEM((layers + 2, window, lanes), jnp.int32),
            pltpu.VMEM((8, lanes), jnp.float32),
            pltpu.VMEM((freqs, 8, lanes), jnp.float32),
            pltpu.VMEM((freqs, 2, layers + 2, window, lanes), jnp.float32),
            pltpu.VMEM((count, layers + 2 * DEPTH, blocks, 2, window, lanes), jnp.float32),
            pltpu.VMEM((num_probes, layers, window, lanes), jnp.float32),
            dma((3, PAIRS)),
            dma((2,)),
            dma((2,)),
            dma((2,)),
            dma((freqs, 2)),
            dma((freqs, PAIRS)),
            dma((freqs,)),
            dma((freqs,)),
            dma((count // DEPTH, 2, blocks)),
            dma((count // DEPTH, 2, blocks)),
            dma((2, 2)),
            dma((2, 2)),
            dma((num_probes, 2)),
            dma((num_probes, PAIRS)),
        ],
        compiler_params=pltpu.CompilerParams(collective_id=0, has_side_effects=True),
    )(shifts, probes, background, medium, receivers)


def solution(mesh):
    in_specs = (
        P(None, "space", None, None),
        P("freq", None, "space", None, None),
        P("space", None, None),
        P("freq", None),
        P("space", None, None),
    )
    out_specs = P(None, "space", "freq", None)
    return jax.shard_map(
        functools.partial(per_device, mesh.shape["freq"], mesh.shape["space"]),
        mesh=mesh, in_specs=in_specs, out_specs=out_specs, check_vma=False,
    )
```

time: 38.8 us -> 35.2 us (0.907)
  Pallas kernels: 37 us -> 33.3 us
    pallas_call x1, Pallas kernels: 37 us -> 33.3 us  [per_device(): pl.pallas_call(functools.partial(kernel, freqs, spaces, rows_all), out_sh...]
where the time goes in v2:
time: 35.2 us; the launch traced here: 34.9 us
  Pallas kernels  33.3 us (95%)
  local copies, waits for them, and re-layouts  1.57 us (4%)
    pallas_call x1, Pallas kernels, per_device(): pl.pallas_call(functools.partial(kernel, freqs, spaces, rows_all), out_sh...  33.3 us
    unnamed x1, local copies, waits for them, and re-layouts  1.57 us

profile of v2, /device:TPU:21, one launch (start us, length us, event | category | flops | bytes accessed | tf_op | source)
XLA Modules:
  0.0 34.9 jit_solution(6562685676993800075)
XLA Ops:
  0.0 33.3 %shard_map.55 = f32[2,2,64,128]{3,2,1,0:T(8,128)} custom-call(f32[1,2]{1,0:T(1,128)} %shifts_ref.1, f32[2,2,128,128]{3,2,1,0:T(8,128)} %probes_ref.1, f32[1,2,2,128,128]{4,3,2,1,0:T(8,128)} %back_ref.1, f32[2,128,128]{2,1,0:T(8,128)} %medium_ref.1, s32[2,128,128]{2,1,0:T(8,128)} %receivers_ref.1), custom_call_target="tpu_custom_call" | custom-call | tf_op jit(solution)/shard_map/pallas_call | solution.py:380
  33.3 1.6 %copy.7 = f32[2,2,64,128]{3,2,1,0:T(8,128)} copy(f32[2,2,64,128]{3,2,1,0:T(8,128)} %shard_map.55) | data formatting | bytes 262144

commit v3 on v2

--- a/solution.py
+++ b/solution.py
@@ -31,9 +31,9 @@
 def kernel(
     freqs, spaces, rows_all, shifts_ref, probes_ref, back_ref, medium_ref, receivers_ref, out_ref,
     probes_in, back_in, medium_in, listen_in, shift_out, shift_in,
-    inverse, fields, terms,
+    inverse, start, fields, terms,
     send_in, recv_probes, recv_medium, recv_listen, recv_back, send_back,
-    send_shift, recv_shift, send_halo, recv_halo, send_near, recv_near, send_out, recv_out,
+    send_shift, recv_shift, send_halo, recv_halo, send_far, recv_far, send_near, recv_near, send_out, recv_out,
 ):
     own = probes_ref.shape[1]
     layers = PAIRS * own
@@ -145,10 +145,11 @@
 
         shared(0, lambda rows: medium_ref.at[:, rows], medium_in.at[mine_near], recv_medium)
         back(h)
-        shared(1, lambda rows: probes_ref.at[:, :, rows], probes_in.at[:, mine], recv_probes)
+        for p in range(num_probes):
+            shared(2 + p, lambda rows: probes_ref.at[p, :, rows], probes_in.at[p, mine], recv_probes.at[p])
+        shared(1, lambda rows: receivers_ref.at[:, rows], listen_in.at[mine_near], recv_listen)
         for turn in range(1, freqs):
             back(lax.rem(h + turn, freqs))
-        shared(2, lambda rows: receivers_ref.at[:, rows], listen_in.at[mine_near], recv_listen)
 
     send_inputs(True)
 
@@ -166,7 +167,17 @@
             else:
                 copy.wait_send()
 
+    inside = pl.ds(pl.multiple_of((h * PAIRS + q) * part - first_row(h, q), 8), part)
+
     def halo(k, block, side, go):
+        if k == sent[-1]:
+            src, dst = (DEPTH, layers + DEPTH) if side == 0 else (layers + 1, 1)
+            send(fields.at[k, src, block], fields.at[k, dst, block],
+                 send_halo.at[k // DEPTH, side, block], recv_halo.at[k // DEPTH, 1 - side, block], side, go)
+            src, dst = (src + 1, dst + 1) if side == 0 else (src - 1, dst - 1)
+            send(fields.at[k, src, block, :, inside], fields.at[k, dst, block, :, inside],
+                 send_far.at[side, block], recv_far.at[1 - side, block], side, go)
+            return
         src = pl.ds(DEPTH if side == 0 else layers, DEPTH)
         dst = pl.ds(layers + DEPTH if side == 0 else 0, DEPTH)
         send(fields.at[k, src, block], fields.at[k, dst, block],
@@ -176,8 +187,13 @@
         for side in range(2):
             @pl.when(has_low if side == 0 else has_high)
             def _():
-                where = pl.ds(0 if side == 0 else layers + DEPTH, DEPTH)
-                arrived(fields.at[k, where, block], recv_halo.at[k // DEPTH, side, block])
+                if k == sent[-1]:
+                    at, far = (1, 0) if side == 0 else (layers + DEPTH, layers + DEPTH + 1)
+                    arrived(fields.at[k, at, block], recv_halo.at[k // DEPTH, side, block])
+                    arrived(fields.at[k, far, block, :, inside], recv_far.at[side, block])
+                else:
+                    where = pl.ds(0 if side == 0 else layers + DEPTH, DEPTH)
+                    arrived(fields.at[k, where, block], recv_halo.at[k // DEPTH, side, block])
 
     def near(ref, index, side, go):
         send(ref.at[1 if side == 0 else layers], ref.at[layers + 1 if side == 0 else 0],
@@ -225,27 +241,34 @@
         for owner in range(2):
             arrived(back_in.at[f, :, pl.ds(owner * own, own)], recv_back.at[f, owner])
 
-        @pl.when(turn == 0)
-        def _():
-            for owner in range(2):
-                arrived(probes_in.at[:, pl.ds(owner * own, own)], recv_probes.at[owner])
-
-        for done, layer in enumerate(order):
-            inv_re, inv_im = invert(f, 1 + layer)
-            scaled_re, scaled_im = scaled(f, layer)
-            start_re = inv_re * scaled_re - inv_im * scaled_im
-            start_im = inv_re * scaled_im + inv_im * scaled_re
-            for p in range(num_probes):
-                block = f * num_probes + p
+        for p in range(num_probes):
+            block = f * num_probes + p
+
+            @pl.when(turn == 0)
+            def _():
+                for owner in range(2):
+                    arrived(probes_in.at[p, pl.ds(owner * own, own)], recv_probes.at[p, owner])
+
+            for done, layer in enumerate(order):
+                if p == 0:
+                    inv_re, inv_im = invert(f, 1 + layer)
+                    scaled_re, scaled_im = scaled(f, layer)
+                    start[0, layer] = inv_re * scaled_re - inv_im * scaled_im
+                    start[1, layer] = inv_re * scaled_im + inv_im * scaled_re
                 probe = probes_in[p, layer]
-                fields[0, DEPTH + layer, block, 0] = start_re * probe
-                fields[0, DEPTH + layer, block, 1] = start_im * probe
+                fields[0, DEPTH + layer, block, 0] = start[0, layer] * probe
+                fields[0, DEPTH + layer, block, 1] = start[1, layer] * probe
                 if done + 1 == ready_low:
                     halo(0, block, 0, True)
                 if done + 1 == ready_high:
                     halo(0, block, 1, True)
 
-    pl.loop(0, freqs)(first)
+    first(0)
+    for owner in range(2):
+        arrived(listen_in.at[pl.ds(1 + owner * own, own)], recv_listen.at[owner])
+    for side in range(2):
+        near(listen_in, 1, side, True)
+    pl.loop(1, freqs)(first)
 
     def update(k, f, block, at, sign):
         new = []
@@ -313,17 +336,9 @@
                     if done + 1 == ready_high:
                         halo(k + DEPTH, block, 1, True)
 
-        if k == 0:
-            for owner in range(2):
-                arrived(listen_in.at[pl.ds(1 + owner * own, own)], recv_listen.at[owner])
-            for side in range(2):
-                near(listen_in, 1, side, True)
-
-    inside = pl.multiple_of((h * PAIRS + q) * part - first_row(h, q), 8)
-
     def send_terms(p, go):
         for owner in range(2):
-            put(terms.at[p, pl.ds(owner * own, own), pl.ds(inside, part)],
+            put(terms.at[p, pl.ds(owner * own, own), inside],
                 out_ref.at[p, :, pl.ds(pl.multiple_of(q * part, 8), part)],
                 send_out.at[p, owner], recv_out.at[p, q], h, base + 2 * c + owner, go)
 
@@ -390,10 +405,11 @@
             pltpu.VMEM((8, lanes), jnp.float32),
             pltpu.VMEM((freqs, 8, lanes), jnp.float32),
             pltpu.VMEM((freqs, 2, layers + 2, window, lanes), jnp.float32),
+            pltpu.VMEM((2, layers, window, lanes), jnp.float32),
             pltpu.VMEM((count, layers + 2 * DEPTH, blocks, 2, window, lanes), jnp.float32),
             pltpu.VMEM((num_probes, layers, window, lanes), jnp.float32),
-            dma((3, PAIRS)),
-            dma((2,)),
+            dma((2 + num_probes, PAIRS)),
+            dma((num_probes, 2)),
             dma((2,)),
             dma((2,)),
             dma((freqs, 2)),
@@ -402,6 +418,8 @@
             dma((freqs,)),
             dma((count // DEPTH, 2, blocks)),
             dma((count // DEPTH, 2, blocks)),
+            dma((2, blocks)),
+            dma((2, blocks)),
             dma((2, 2)),
             dma((2, 2)),
             dma((num_probes, 2)),

time: 35.2 us -> 32.7 us (0.929)
  Pallas kernels: 33.3 us -> 30.8 us
    pallas_call x1, Pallas kernels: 33.3 us -> 30.8 us  [per_device(): pl.pallas_call(functools.partial(kernel, freqs, spaces, rows_all), out_sh...]
where the time goes in v3:
time: 32.7 us; the launch traced here: 32.4 us
  Pallas kernels  30.8 us (94%)
  local copies, waits for them, and re-layouts  1.57 us (5%)
    pallas_call x1, Pallas kernels, per_device(): pl.pallas_call(functools.partial(kernel, freqs, spaces, rows_all), out_sh...  30.8 us
    unnamed x1, local copies, waits for them, and re-layouts  1.57 us

profile of v3, /device:TPU:21, one launch (start us, length us, event | category | flops | bytes accessed | tf_op | source)
XLA Modules:
  0.0 32.4 jit_solution(17294512786418751973)
XLA Ops:
  0.0 30.8 %shard_map.55 = f32[2,2,64,128]{3,2,1,0:T(8,128)} custom-call(f32[1,2]{1,0:T(1,128)} %shifts_ref.1, f32[2,2,128,128]{3,2,1,0:T(8,128)} %probes_ref.1, f32[1,2,2,128,128]{4,3,2,1,0:T(8,128)} %back_ref.1, f32[2,128,128]{2,1,0:T(8,128)} %medium_ref.1, s32[2,128,128]{2,1,0:T(8,128)} %receivers_ref.1), custom_call_target="tpu_custom_call" | custom-call | tf_op jit(solution)/shard_map/pallas_call | solution.py:395
  30.8 1.6 %copy.7 = f32[2,2,64,128]{3,2,1,0:T(8,128)} copy(f32[2,2,64,128]{3,2,1,0:T(8,128)} %shard_map.55) | data formatting | bytes 262144

commit v4 on v3

--- a/solution.py
+++ b/solution.py
@@ -31,7 +31,7 @@
 def kernel(
     freqs, spaces, rows_all, shifts_ref, probes_ref, back_ref, medium_ref, receivers_ref, out_ref,
     probes_in, back_in, medium_in, listen_in, shift_out, shift_in,
-    inverse, start, fields, terms,
+    inverse, start, margin_out, margin_in, fields, terms,
     send_in, recv_probes, recv_medium, recv_listen, recv_back, send_back,
     send_shift, recv_shift, send_halo, recv_halo, send_far, recv_far, send_near, recv_near, send_out, recv_out,
 ):
@@ -167,33 +167,60 @@
             else:
                 copy.wait_send()
 
-    inside = pl.ds(pl.multiple_of((h * PAIRS + q) * part - first_row(h, q), 8), part)
+    inside_at = pl.multiple_of((h * PAIRS + q) * part - first_row(h, q), 8)
+    inside = pl.ds(inside_at, part)
+    tile_low = pl.ds(pl.multiple_of(jnp.maximum(inside_at - 8, 0), 8), 8)
+    tile_high = pl.ds(pl.multiple_of(jnp.minimum(inside_at + part, window - 8), 8), 8)
+
+    def margin_items(k, side, src_side):
+        if k == sent[-1]:
+            if src_side:
+                return ((2, DEPTH if side == 0 else layers + 1),)
+            return ((2, 1 if side == 0 else layers + DEPTH),)
+        first_layer = (DEPTH if side == 0 else layers) if src_side else (0 if side == 0 else layers + DEPTH)
+        return tuple((item, first_layer + item) for item in range(DEPTH))
 
     def halo(k, block, side, go):
-        if k == sent[-1]:
-            src, dst = (DEPTH, layers + DEPTH) if side == 0 else (layers + 1, 1)
+        src = pl.ds(DEPTH if side == 0 else layers, DEPTH)
+        dst = pl.ds(layers + DEPTH if side == 0 else 0, DEPTH)
+        if k == 0:
             send(fields.at[k, src, block], fields.at[k, dst, block],
                  send_halo.at[k // DEPTH, side, block], recv_halo.at[k // DEPTH, 1 - side, block], side, go)
-            src, dst = (src + 1, dst + 1) if side == 0 else (src - 1, dst - 1)
-            send(fields.at[k, src, block, :, inside], fields.at[k, dst, block, :, inside],
-                 send_far.at[side, block], recv_far.at[1 - side, block], side, go)
             return
-        src = pl.ds(DEPTH if side == 0 else layers, DEPTH)
-        dst = pl.ds(layers + DEPTH if side == 0 else 0, DEPTH)
-        send(fields.at[k, src, block], fields.at[k, dst, block],
+        items = margin_items(k, side, True)
+        if go:
+            for item, at in items:
+                for part_of in range(2):
+                    low_rows = fields[k, at, block, part_of, tile_low]
+                    high_rows = fields[k, at, block, part_of, tile_high]
+                    row = lax.broadcasted_iota(jnp.int32, low_rows.shape, 0)
+                    margin_out[side, block, item, part_of] = jnp.where(row < 4, high_rows, low_rows)
+        send(fields.at[k, src, block, :, inside], fields.at[k, dst, block, :, inside],
              send_halo.at[k // DEPTH, side, block], recv_halo.at[k // DEPTH, 1 - side, block], side, go)
+        which = pl.ds(items[0][0], len(items))
+        send(margin_out.at[side, block, which], margin_in.at[1 - side, block, which],
+             send_far.at[k // DEPTH, side, block], recv_far.at[k // DEPTH, 1 - side, block], side, go)
 
     def halo_arrived(k, block):
         for side in range(2):
             @pl.when(has_low if side == 0 else has_high)
             def _():
-                if k == sent[-1]:
-                    at, far = (1, 0) if side == 0 else (layers + DEPTH, layers + DEPTH + 1)
-                    arrived(fields.at[k, at, block], recv_halo.at[k // DEPTH, side, block])
-                    arrived(fields.at[k, far, block, :, inside], recv_far.at[side, block])
-                else:
-                    where = pl.ds(0 if side == 0 else layers + DEPTH, DEPTH)
+                where = pl.ds(0 if side == 0 else layers + DEPTH, DEPTH)
+                if k == 0:
                     arrived(fields.at[k, where, block], recv_halo.at[k // DEPTH, side, block])
+                    return
+                items = margin_items(k, side, False)
+                which = pl.ds(items[0][0], len(items))
+                arrived(fields.at[k, where, block, :, inside], recv_halo.at[k // DEPTH, side, block])
+                arrived(margin_in.at[side, block, which], recv_far.at[k // DEPTH, side, block])
+                for item, at in items:
+                    @pl.when(inside_at >= 8)
+                    def _():
+                        fields[k, at, block, :, tile_low] = margin_in[side, block, item]
+
+                    @pl.when(inside_at + part <= window - 8)
+                    def _():
+                        fields[k, at, block, :, tile_high] = margin_in[side, block, item]
 
     def near(ref, index, side, go):
         send(ref.at[1 if side == 0 else layers], ref.at[layers + 1 if side == 0 else 0],
@@ -406,6 +433,8 @@
             pltpu.VMEM((freqs, 8, lanes), jnp.float32),
             pltpu.VMEM((freqs, 2, layers + 2, window, lanes), jnp.float32),
             pltpu.VMEM((2, layers, window, lanes), jnp.float32),
+            pltpu.VMEM((2, blocks, 3, 2, 8, lanes), jnp.float32),
+            pltpu.VMEM((2, blocks, 3, 2, 8, lanes), jnp.float32),
             pltpu.VMEM((count, layers + 2 * DEPTH, blocks, 2, window, lanes), jnp.float32),
             pltpu.VMEM((num_probes, layers, window, lanes), jnp.float32),
             dma((2 + num_probes, PAIRS)),
@@ -418,8 +447,8 @@
             dma((freqs,)),
             dma((count // DEPTH, 2, blocks)),
             dma((count // DEPTH, 2, blocks)),
-            dma((2, blocks)),
-            dma((2, blocks)),
+            dma((count // DEPTH, 2, blocks)),
+            dma((count // DEPTH, 2, blocks)),
             dma((2, 2)),
             dma((2, 2)),
             dma((num_probes, 2)),

time: 32.7 us -> 32.3 us (0.988)
  Pallas kernels: 30.8 us -> 30.3 us
    pallas_call x1, Pallas kernels: 30.8 us -> 30.3 us  [per_device(): pl.pallas_call(functools.partial(kernel, freqs, spaces, rows_all), out_sh...]
where the time goes in v4:
time: 32.3 us; the launch traced here: 31.9 us
  Pallas kernels  30.3 us (94%)
  local copies, waits for them, and re-layouts  1.57 us (5%)
    pallas_call x1, Pallas kernels, per_device(): pl.pallas_call(functools.partial(kernel, freqs, spaces, rows_all), out_sh...  30.3 us
    unnamed x1, local copies, waits for them, and re-layouts  1.57 us

profile of v4, /device:TPU:21, one launch (start us, length us, event | category | flops | bytes accessed | tf_op | source)
XLA Modules:
  0.0 31.9 jit_solution(12451360080890640143)
XLA Ops:
  0.0 30.3 %shard_map.55 = f32[2,2,64,128]{3,2,1,0:T(8,128)} custom-call(f32[1,2]{1,0:T(1,128)} %shifts_ref.1, f32[2,2,128,128]{3,2,1,0:T(8,128)} %probes_ref.1, f32[1,2,2,128,128]{4,3,2,1,0:T(8,128)} %back_ref.1, f32[2,128,128]{2,1,0:T(8,128)} %medium_ref.1, s32[2,128,128]{2,1,0:T(8,128)} %receivers_ref.1), custom_call_target="tpu_custom_call" | custom-call | tf_op jit(solution)/shard_map/pallas_call | solution.py:422
  30.3 1.6 %copy.7 = f32[2,2,64,128]{3,2,1,0:T(8,128)} copy(f32[2,2,64,128]{3,2,1,0:T(8,128)} %shard_map.55) | data formatting | bytes 262144
